TPU v7x, 128 devices: a whole 4x4x4 slice. The times are simulated.
128 devices in a mesh: row: 8 (over y_hi, z), col: 16 (over y_lo, x, core).
Axes of the slice: x: 4, y: 4 (y_hi: 2, y_lo: 2; y = y_hi * 2 + y_lo), z: 4, core: 2. Of those that a mesh axis runs over, the one named last changes fastest.
Arguments:
- a_tiles: float32 [8, 16, 8, 128, 128], P('row', 'col'), may hold values from -6 to 6
- b_tiles: float32 [8, 16, 8, 128, 128], P('row', 'col'), may hold values from -0.25 to 0.25
- pair_lists: int32 [8, 16, 16, 3, 32], P('row', 'col'), may hold values from 0 to 63, as said below
- stack_counts: int32 [8, 16, 16], P('row', 'col'), may hold values from 1 to 32, as said below
Outputs:
- c_tiles: float32 [8, 16, 32, 128, 128], P('row', 'col')
Inputs may be any that keep to these rules, and one draw needn't show every extreme that they name: `pair_lists`: entry 0 of a list column is an A tile slot below 8, entry 1 a tile of bcol below 64, entry 2 a product tile below 32; entries past the live count are valid indices that do not count. `stack_counts`: live entries of each list; in every draw some list has all 32 live.
All inputs are finite; a program needn't handle non-finite values.
Results may differ from a plain program's by a relative error of at most 0.0003.
Values sent between devices are 32-bit elements; how exact they have to be, the bound alone decides.
No kernel may reach another device: no remote copies, remote signals or barrier semaphores. Data moves between devices by JAX's collectives and lax.ppermute only.
A program may use at most 64 MiB of HBM per device.

v0:
```python
import math
import jax
import jax.numpy as jnp
from jax import lax
from jax.sharding import PartitionSpec as P

CT = 32


def shifted(value, axis, steps):
    count = lax.axis_size(axis)
    pairs = [(source, (source + steps) % count) for source in range(count)]
    return lax.ppermute(value, axis, pairs)


def add_block(totals, a_panel, b_all, stack_list, count_live, group_size):
    is_live = jnp.arange(group_size, dtype=jnp.int32) < count_live
    a_pick = (
        stack_list[0][:, None] == jnp.arange(a_panel.shape[0], dtype=jnp.int32)[None, :]
    ).astype(jnp.float32)
    b_pick = (
        stack_list[1][:, None] == jnp.arange(b_all.shape[0], dtype=jnp.int32)[None, :]
    ).astype(jnp.float32)
    c_place = (
        jnp.arange(totals.shape[0], dtype=jnp.int32)[:, None] == stack_list[2][None, :]
    ) & is_live[None, :]
    c_place = c_place.astype(jnp.float32)
    left_tiles = jnp.einsum(
        "gs,sij->gij",
        a_pick,
        a_panel,
        precision=lax.Precision.HIGHEST,
        preferred_element_type=jnp.float32,
    )
    right_tiles = jnp.einsum(
        "gs,sij->gij",
        b_pick,
        b_all,
        precision=lax.Precision.HIGHEST,
        preferred_element_type=jnp.float32,
    )
    products = jnp.einsum(
        "gij,gjk->gik",
        left_tiles,
        right_tiles,
        precision=lax.Precision.HIGHEST,
        preferred_element_type=jnp.float32,
    )
    return totals + jnp.einsum(
        "mg,gik->mik",
        c_place,
        products,
        precision=lax.Precision.HIGHEST,
        preferred_element_type=jnp.float32,
    )


def apply_panel(totals, a_panel, b_all, stack_list, count_live):
    entries = stack_list.shape[1]
    group_size = math.gcd(entries, 32)
    totals = add_block(totals, a_panel, b_all, stack_list, count_live, group_size)
    return totals


def body(a_tiles, b_tiles, pair_lists, stack_counts):
    tile_width = a_tiles.shape[3]
    col_count = lax.axis_size("col")
    own_column = lax.axis_index("col")
    gathered_b = lax.all_gather(b_tiles, "row", axis=0, tiled=True)
    b_all = gathered_b.reshape(-1, tile_width, tile_width)
    lists_all = pair_lists[0, 0]
    counts_all = stack_counts[0, 0]

    def visit(totals, a_panel, panel_index, keep_flag):
        stack_list = lax.dynamic_index_in_dim(lists_all, panel_index, 0, keepdims=False)
        count_live = (
            lax.dynamic_index_in_dim(counts_all, panel_index, 0, keepdims=False) * keep_flag
        )
        return apply_panel(totals, a_panel, b_all, stack_list, count_live)

    totals = jnp.zeros((CT, tile_width, tile_width), jnp.float32)
    own_panel = a_tiles[0, 0]
    totals = visit(totals, own_panel, own_column, 1)

    def next_stop(stop_index, loop_state):
        totals_in, moving = loop_state
        moving = shifted(moving, "col", 1)
        panel_index = (own_column - stop_index) % col_count
        return (visit(totals_in, moving, panel_index, 1), moving)

    totals, moving = lax.fori_loop(1, col_count, next_stop, (totals, own_panel))
    return totals[None, None]


def solution(mesh):
    return jax.shard_map(
        body,
        mesh=mesh,
        in_specs=(
            P("row", "col", None, None, None),
            P("row", "col", None, None, None),
            P("row", "col", None, None, None),
            P("row", "col", None),
        ),
        out_specs=P("row", "col", None, None, None),
        check_vma=False,
    )
```

profile of v0, /device:TPU:0, one launch (start us, length us, event | category | flops | bytes accessed | tf_op | source)
XLA Modules:
  0.0 401.2 jit_solution(11839348177748028509)
XLA Ops:
  12.1 71.7 %all-gather.2.cloned.1.call-done = f32[8,1,8,128,128]{4,3,2,1,0:T(8,128)} async-done(((f32[1,1,8,128,128]{4,3,2,1,0:T(8,128)}), f32[8,1,8,128,128]{4,3,2,1,0:T(8,128)}) %all-gather.2.cloned.1.call-update) | async-done | bytes 4194320 | tf_op jit(solution)/shard_map/all_gather | solution.py:69
  83.8 6.1 %fusion.23 = f32[32,128,128]{2,0,1:T(8,128)S(1)} fusion(f32[64,128,128]{2,1,0:T(8,128)} %bitcast.51, s32[32]{0:T(128)S(1)} %get-tuple-element.202), kind=kOutput, calls=%fused_computation.26 | convolution fusion | flops 402655232 | bytes 6291584 | tf_op jit(solution)/shard_map/gs,sij->gij/dot_general | solution.py:35
  96.9 294.9 %while.17 = (s32[]{:T(128)}, f32[32,128,128]{2,0,1:T(8,128)S(1)}, f32[8,128,128]{2,1,0:T(8,128)S(1)}, s32[]{:T(128)}, s32[16,3,32]{2,1,0:T(4,128)S(1)}, /*index=...) while((s32[]{:T(128)}, f32[32,128,128]{2,0,1:T(8,128)S(1)}, ...), condition=%wide.region_1.2_spmd, body=%wide.region_0.1_spmd.sunk | while | flops 1460146432 | bytes 24643844 | solution.py:91
  98.4 6.1 %fusion.66 = f32[32,128,128]{2,0,1:T(8,128)S(1)} fusion(f32[64,128,128]{2,1,0:T(8,128)} %get-tuple-element.280, s32[32]{0:T(128)S(1)} %get-tuple-element.249), kind=kOutput, calls=%fused_computation.clone.1 | convolution fusion | flops 402655232 | bytes 6291584 | tf_op jit(solution)/shard_map/while/body/eval_jaxpr/gs,sij->gij/dot_general | solution.py:35
  108.9 4.6 %fusion.68 = f32[32,128,128]{2,1,0:T(8,128)S(1)} fusion(f32[32,128,128]{2,0,1:T(8,128)S(1)} %fusion.66, f32[32,128,128]{2,0,1:T(8,128)S(1)} %fusion.67), kind=kOutput, calls=%fused_computation.4.clone.1 | convolution fusion | flops 805306368 | bytes 6291456 | tf_op jit(solution)/shard_map/while/body/eval_jaxpr/gij,gjk->gik/dot_general | solution.py:42
  118.1 6.1 %fusion.66 = f32[32,128,128]{2,0,1:T(8,128)S(1)} fusion(f32[64,128,128]{2,1,0:T(8,128)} %get-tuple-element.280, s32[32]{0:T(128)S(1)} %get-tuple-element.249), kind=kOutput, calls=%fused_computation.clone.1 | convolution fusion | flops 402655232 | bytes 6291584 | tf_op jit(solution)/shard_map/while/body/eval_jaxpr/gs,sij->gij/dot_general | solution.py:35
  128.6 4.6 %fusion.68 = f32[32,128,128]{2,1,0:T(8,128)S(1)} fusion(f32[32,128,128]{2,0,1:T(8,128)S(1)} %fusion.66, f32[32,128,128]{2,0,1:T(8,128)S(1)} %fusion.67), kind=kOutput, calls=%fused_computation.4.clone.1 | convolution fusion | flops 805306368 | bytes 6291456 | tf_op jit(solution)/shard_map/while/body/eval_jaxpr/gij,gjk->gik/dot_general | solution.py:42
  137.7 6.1 %fusion.66 = f32[32,128,128]{2,0,1:T(8,128)S(1)} fusion(f32[64,128,128]{2,1,0:T(8,128)} %get-tuple-element.280, s32[32]{0:T(128)S(1)} %get-tuple-element.249), kind=kOutput, calls=%fused_computation.clone.1 | convolution fusion | flops 402655232 | bytes 6291584 | tf_op jit(solution)/shard_map/while/body/eval_jaxpr/gs,sij->gij/dot_general | solution.py:35
  148.2 4.6 %fusion.68 = f32[32,128,128]{2,1,0:T(8,128)S(1)} fusion(f32[32,128,128]{2,0,1:T(8,128)S(1)} %fusion.66, f32[32,128,128]{2,0,1:T(8,128)S(1)} %fusion.67), kind=kOutput, calls=%fused_computation.4.clone.1 | convolution fusion | flops 805306368 | bytes 6291456 | tf_op jit(solution)/shard_map/while/body/eval_jaxpr/gij,gjk->gik/dot_general | solution.py:42
  157.4 6.1 %fusion.66 = f32[32,128,128]{2,0,1:T(8,128)S(1)} fusion(f32[64,128,128]{2,1,0:T(8,128)} %get-tuple-element.280, s32[32]{0:T(128)S(1)} %get-tuple-element.249), kind=kOutput, calls=%fused_computation.clone.1 | convolution fusion | flops 402655232 | bytes 6291584 | tf_op jit(solution)/shard_map/while/body/eval_jaxpr/gs,sij->gij/dot_general | solution.py:35
  167.9 4.6 %fusion.68 = f32[32,128,128]{2,1,0:T(8,128)S(1)} fusion(f32[32,128,128]{2,0,1:T(8,128)S(1)} %fusion.66, f32[32,128,128]{2,0,1:T(8,128)S(1)} %fusion.67), kind=kOutput, calls=%fused_computation.4.clone.1 | convolution fusion | flops 805306368 | bytes 6291456 | tf_op jit(solution)/shard_map/while/body/eval_jaxpr/gij,gjk->gik/dot_general | solution.py:42
  177.0 6.1 %fusion.66 = f32[32,128,128]{2,0,1:T(8,128)S(1)} fusion(f32[64,128,128]{2,1,0:T(8,128)} %get-tuple-element.280, s32[32]{0:T(128)S(1)} %get-tuple-element.249), kind=kOutput, calls=%fused_computation.clone.1 | convolution fusion | flops 402655232 | bytes 6291584 | tf_op jit(solution)/shard_map/while/body/eval_jaxpr/gs,sij->gij/dot_general | solution.py:35
  187.5 4.6 %fusion.68 = f32[32,128,128]{2,1,0:T(8,128)S(1)} fusion(f32[32,128,128]{2,0,1:T(8,128)S(1)} %fusion.66, f32[32,128,128]{2,0,1:T(8,128)S(1)} %fusion.67), kind=kOutput, calls=%fused_computation.4.clone.1 | convolution fusion | flops 805306368 | bytes 6291456 | tf_op jit(solution)/shard_map/while/body/eval_jaxpr/gij,gjk->gik/dot_general | solution.py:42
  196.7 6.1 %fusion.66 = f32[32,128,128]{2,0,1:T(8,128)S(1)} fusion(f32[64,128,128]{2,1,0:T(8,128)} %get-tuple-element.280, s32[32]{0:T(128)S(1)} %get-tuple-element.249), kind=kOutput, calls=%fused_computation.clone.1 | convolution fusion | flops 402655232 | bytes 6291584 | tf_op jit(solution)/shard_map/while/body/eval_jaxpr/gs,sij->gij/dot_general | solution.py:35
  207.2 4.6 %fusion.68 = f32[32,128,128]{2,1,0:T(8,128)S(1)} fusion(f32[32,128,128]{2,0,1:T(8,128)S(1)} %fusion.66, f32[32,128,128]{2,0,1:T(8,128)S(1)} %fusion.67), kind=kOutput, calls=%fused_computation.4.clone.1 | convolution fusion | flops 805306368 | bytes 6291456 | tf_op jit(solution)/shard_map/while/body/eval_jaxpr/gij,gjk->gik/dot_general | solution.py:42
  216.3 6.1 %fusion.66 = f32[32,128,128]{2,0,1:T(8,128)S(1)} fusion(f32[64,128,128]{2,1,0:T(8,128)} %get-tuple-element.280, s32[32]{0:T(128)S(1)} %get-tuple-element.249), kind=kOutput, calls=%fused_computation.clone.1 | convolution fusion | flops 402655232 | bytes 6291584 | tf_op jit(solution)/shard_map/while/body/eval_jaxpr/gs,sij->gij/dot_general | solution.py:35
  226.8 4.6 %fusion.68 = f32[32,128,128]{2,1,0:T(8,128)S(1)} fusion(f32[32,128,128]{2,0,1:T(8,128)S(1)} %fusion.66, f32[32,128,128]{2,0,1:T(8,128)S(1)} %fusion.67), kind=kOutput, calls=%fused_computation.4.clone.1 | convolution fusion | flops 805306368 | bytes 6291456 | tf_op jit(solution)/shard_map/while/body/eval_jaxpr/gij,gjk->gik/dot_general | solution.py:42
  236.0 6.1 %fusion.66 = f32[32,128,128]{2,0,1:T(8,128)S(1)} fusion(f32[64,128,128]{2,1,0:T(8,128)} %get-tuple-element.280, s32[32]{0:T(128)S(1)} %get-tuple-element.249), kind=kOutput, calls=%fused_computation.clone.1 | convolution fusion | flops 402655232 | bytes 6291584 | tf_op jit(solution)/shard_map/while/body/eval_jaxpr/gs,sij->gij/dot_general | solution.py:35
  246.5 4.6 %fusion.68 = f32[32,128,128]{2,1,0:T(8,128)S(1)} fusion(f32[32,128,128]{2,0,1:T(8,128)S(1)} %fusion.66, f32[32,128,128]{2,0,1:T(8,128)S(1)} %fusion.67), kind=kOutput, calls=%fused_computation.4.clone.1 | convolution fusion | flops 805306368 | bytes 6291456 | tf_op jit(solution)/shard_map/while/body/eval_jaxpr/gij,gjk->gik/dot_general | solution.py:42
  255.6 6.1 %fusion.66 = f32[32,128,128]{2,0,1:T(8,128)S(1)} fusion(f32[64,128,128]{2,1,0:T(8,128)} %get-tuple-element.280, s32[32]{0:T(128)S(1)} %get-tuple-element.249), kind=kOutput, calls=%fused_computation.clone.1 | convolution fusion | flops 402655232 | bytes 6291584 | tf_op jit(solution)/shard_map/while/body/eval_jaxpr/gs,sij->gij/dot_general | solution.py:35
  266.1 4.6 %fusion.68 = f32[32,128,128]{2,1,0:T(8,128)S(1)} fusion(f32[32,128,128]{2,0,1:T(8,128)S(1)} %fusion.66, f32[32,128,128]{2,0,1:T(8,128)S(1)} %fusion.67), kind=kOutput, calls=%fused_computation.4.clone.1 | convolution fusion | flops 805306368 | bytes 6291456 | tf_op jit(solution)/shard_map/while/body/eval_jaxpr/gij,gjk->gik/dot_general | solution.py:42
  275.3 6.1 %fusion.66 = f32[32,128,128]{2,0,1:T(8,128)S(1)} fusion(f32[64,128,128]{2,1,0:T(8,128)} %get-tuple-element.280, s32[32]{0:T(128)S(1)} %get-tuple-element.249), kind=kOutput, calls=%fused_computation.clone.1 | convolution fusion | flops 402655232 | bytes 6291584 | tf_op jit(solution)/shard_map/while/body/eval_jaxpr/gs,sij->gij/dot_general | solution.py:35
  285.8 4.6 %fusion.68 = f32[32,128,128]{2,1,0:T(8,128)S(1)} fusion(f32[32,128,128]{2,0,1:T(8,128)S(1)} %fusion.66, f32[32,128,128]{2,0,1:T(8,128)S(1)} %fusion.67), kind=kOutput, calls=%fused_computation.4.clone.1 | convolution fusion | flops 805306368 | bytes 6291456 | tf_op jit(solution)/shard_map/while/body/eval_jaxpr/gij,gjk->gik/dot_general | solution.py:42
  294.9 6.1 %fusion.66 = f32[32,128,128]{2,0,1:T(8,128)S(1)} fusion(f32[64,128,128]{2,1,0:T(8,128)} %get-tuple-element.280, s32[32]{0:T(128)S(1)} %get-tuple-element.249), kind=kOutput, calls=%fused_computation.clone.1 | convolution fusion | flops 402655232 | bytes 6291584 | tf_op jit(solution)/shard_map/while/body/eval_jaxpr/gs,sij->gij/dot_general | solution.py:35
  305.4 4.6 %fusion.68 = f32[32,128,128]{2,1,0:T(8,128)S(1)} fusion(f32[32,128,128]{2,0,1:T(8,128)S(1)} %fusion.66, f32[32,128,128]{2,0,1:T(8,128)S(1)} %fusion.67), kind=kOutput, calls=%fused_computation.4.clone.1 | convolution fusion | flops 805306368 | bytes 6291456 | tf_op jit(solution)/shard_map/while/body/eval_jaxpr/gij,gjk->gik/dot_general | solution.py:42
  314.6 6.1 %fusion.66 = f32[32,128,128]{2,0,1:T(8,128)S(1)} fusion(f32[64,128,128]{2,1,0:T(8,128)} %get-tuple-element.280, s32[32]{0:T(128)S(1)} %get-tuple-element.249), kind=kOutput, calls=%fused_computation.clone.1 | convolution fusion | flops 402655232 | bytes 6291584 | tf_op jit(solution)/shard_map/while/body/eval_jaxpr/gs,sij->gij/dot_general | solution.py:35
  325.1 4.6 %fusion.68 = f32[32,128,128]{2,1,0:T(8,128)S(1)} fusion(f32[32,128,128]{2,0,1:T(8,128)S(1)} %fusion.66, f32[32,128,128]{2,0,1:T(8,128)S(1)} %fusion.67), kind=kOutput, calls=%fused_computation.4.clone.1 | convolution fusion | flops 805306368 | bytes 6291456 | tf_op jit(solution)/shard_map/while/body/eval_jaxpr/gij,gjk->gik/dot_general | solution.py:42
  334.2 6.1 %fusion.66 = f32[32,128,128]{2,0,1:T(8,128)S(1)} fusion(f32[64,128,128]{2,1,0:T(8,128)} %get-tuple-element.280, s32[32]{0:T(128)S(1)} %get-tuple-element.249), kind=kOutput, calls=%fused_computation.clone.1 | convolution fusion | flops 402655232 | bytes 6291584 | tf_op jit(solution)/shard_map/while/body/eval_jaxpr/gs,sij->gij/dot_general | solution.py:35
  344.7 4.6 %fusion.68 = f32[32,128,128]{2,1,0:T(8,128)S(1)} fusion(f32[32,128,128]{2,0,1:T(8,128)S(1)} %fusion.66, f32[32,128,128]{2,0,1:T(8,128)S(1)} %fusion.67), kind=kOutput, calls=%fused_computation.4.clone.1 | convolution fusion | flops 805306368 | bytes 6291456 | tf_op jit(solution)/shard_map/while/body/eval_jaxpr/gij,gjk->gik/dot_general | solution.py:42
  353.8 6.1 %fusion.66 = f32[32,128,128]{2,0,1:T(8,128)S(1)} fusion(f32[64,128,128]{2,1,0:T(8,128)} %get-tuple-element.280, s32[32]{0:T(128)S(1)} %get-tuple-element.249), kind=kOutput, calls=%fused_computation.clone.1 | convolution fusion | flops 402655232 | bytes 6291584 | tf_op jit(solution)/shard_map/while/body/eval_jaxpr/gs,sij->gij/dot_general | solution.py:35
  364.4 4.6 %fusion.68 = f32[32,128,128]{2,1,0:T(8,128)S(1)} fusion(f32[32,128,128]{2,0,1:T(8,128)S(1)} %fusion.66, f32[32,128,128]{2,0,1:T(8,128)S(1)} %fusion.67), kind=kOutput, calls=%fused_computation.4.clone.1 | convolution fusion | flops 805306368 | bytes 6291456 | tf_op jit(solution)/shard_map/while/body/eval_jaxpr/gij,gjk->gik/dot_general | solution.py:42
  373.5 6.1 %fusion.66 = f32[32,128,128]{2,0,1:T(8,128)S(1)} fusion(f32[64,128,128]{2,1,0:T(8,128)} %get-tuple-element.280, s32[32]{0:T(128)S(1)} %get-tuple-element.249), kind=kOutput, calls=%fused_computation.clone.1 | convolution fusion | flops 402655232 | bytes 6291584 | tf_op jit(solution)/shard_map/while/body/eval_jaxpr/gs,sij->gij/dot_general | solution.py:35
  (149 shorter events, 153.2 us)
Async XLA Ops:
  6.5 77.3 %all-gather.2.cloned.1.call-start = ((), (), s32[]{:S(2)}) async-start(), calls=%async_computation | async-start | bytes 4718592 | tf_op jit(solution)/shard_map/all_gather | solution.py:69
  94.4 2.4 copy-start
  97.1 10.8 %collective-permute-start = (f32[8,128,128]{2,1,0:T(8,128)S(1)}, f32[8,128,128]{2,1,0:T(8,128)S(1)}, u32[]{:S(2)}, u32[]{:S(2)}) collective-permute-start(f32[8,128,128]{2,1,0:T(8,128)S(1)} %get-tuple-element.265), channel_id=1, source_target_pairs={{0,1},{1,2},{2,3},{3,4},{4,5},{5,6},{6,7},{7,8},{8,9},{9,10},{10,1... | collective-permute-start | bytes 1572872 | tf_op jit(solution)/shard_map/while/body/eval_jaxpr/ppermute | solution.py:13
  116.7 10.8 %collective-permute-start = (f32[8,128,128]{2,1,0:T(8,128)S(1)}, f32[8,128,128]{2,1,0:T(8,128)S(1)}, u32[]{:S(2)}, u32[]{:S(2)}) collective-permute-start(f32[8,128,128]{2,1,0:T(8,128)S(1)} %get-tuple-element.265), channel_id=1, source_target_pairs={{0,1},{1,2},{2,3},{3,4},{4,5},{5,6},{6,7},{7,8},{8,9},{9,10},{10,1... | collective-permute-start | bytes 1572872 | tf_op jit(solution)/shard_map/while/body/eval_jaxpr/ppermute | solution.py:13
  136.4 10.8 %collective-permute-start = (f32[8,128,128]{2,1,0:T(8,128)S(1)}, f32[8,128,128]{2,1,0:T(8,128)S(1)}, u32[]{:S(2)}, u32[]{:S(2)}) collective-permute-start(f32[8,128,128]{2,1,0:T(8,128)S(1)} %get-tuple-element.265), channel_id=1, source_target_pairs={{0,1},{1,2},{2,3},{3,4},{4,5},{5,6},{6,7},{7,8},{8,9},{9,10},{10,1... | collective-permute-start | bytes 1572872 | tf_op jit(solution)/shard_map/while/body/eval_jaxpr/ppermute | solution.py:13
  156.0 10.8 %collective-permute-start = (f32[8,128,128]{2,1,0:T(8,128)S(1)}, f32[8,128,128]{2,1,0:T(8,128)S(1)}, u32[]{:S(2)}, u32[]{:S(2)}) collective-permute-start(f32[8,128,128]{2,1,0:T(8,128)S(1)} %get-tuple-element.265), channel_id=1, source_target_pairs={{0,1},{1,2},{2,3},{3,4},{4,5},{5,6},{6,7},{7,8},{8,9},{9,10},{10,1... | collective-permute-start | bytes 1572872 | tf_op jit(solution)/shard_map/while/body/eval_jaxpr/ppermute | solution.py:13
  175.7 10.8 %collective-permute-start = (f32[8,128,128]{2,1,0:T(8,128)S(1)}, f32[8,128,128]{2,1,0:T(8,128)S(1)}, u32[]{:S(2)}, u32[]{:S(2)}) collective-permute-start(f32[8,128,128]{2,1,0:T(8,128)S(1)} %get-tuple-element.265), channel_id=1, source_target_pairs={{0,1},{1,2},{2,3},{3,4},{4,5},{5,6},{6,7},{7,8},{8,9},{9,10},{10,1... | collective-permute-start | bytes 1572872 | tf_op jit(solution)/shard_map/while/body/eval_jaxpr/ppermute | solution.py:13
  195.3 10.8 %collective-permute-start = (f32[8,128,128]{2,1,0:T(8,128)S(1)}, f32[8,128,128]{2,1,0:T(8,128)S(1)}, u32[]{:S(2)}, u32[]{:S(2)}) collective-permute-start(f32[8,128,128]{2,1,0:T(8,128)S(1)} %get-tuple-element.265), channel_id=1, source_target_pairs={{0,1},{1,2},{2,3},{3,4},{4,5},{5,6},{6,7},{7,8},{8,9},{9,10},{10,1... | collective-permute-start | bytes 1572872 | tf_op jit(solution)/shard_map/while/body/eval_jaxpr/ppermute | solution.py:13
  215.0 10.8 %collective-permute-start = (f32[8,128,128]{2,1,0:T(8,128)S(1)}, f32[8,128,128]{2,1,0:T(8,128)S(1)}, u32[]{:S(2)}, u32[]{:S(2)}) collective-permute-start(f32[8,128,128]{2,1,0:T(8,128)S(1)} %get-tuple-element.265), channel_id=1, source_target_pairs={{0,1},{1,2},{2,3},{3,4},{4,5},{5,6},{6,7},{7,8},{8,9},{9,10},{10,1... | collective-permute-start | bytes 1572872 | tf_op jit(solution)/shard_map/while/body/eval_jaxpr/ppermute | solution.py:13
  234.6 10.8 %collective-permute-start = (f32[8,128,128]{2,1,0:T(8,128)S(1)}, f32[8,128,128]{2,1,0:T(8,128)S(1)}, u32[]{:S(2)}, u32[]{:S(2)}) collective-permute-start(f32[8,128,128]{2,1,0:T(8,128)S(1)} %get-tuple-element.265), channel_id=1, source_target_pairs={{0,1},{1,2},{2,3},{3,4},{4,5},{5,6},{6,7},{7,8},{8,9},{9,10},{10,1... | collective-permute-start | bytes 1572872 | tf_op jit(solution)/shard_map/while/body/eval_jaxpr/ppermute | solution.py:13
  254.3 10.8 %collective-permute-start = (f32[8,128,128]{2,1,0:T(8,128)S(1)}, f32[8,128,128]{2,1,0:T(8,128)S(1)}, u32[]{:S(2)}, u32[]{:S(2)}) collective-permute-start(f32[8,128,128]{2,1,0:T(8,128)S(1)} %get-tuple-element.265), channel_id=1, source_target_pairs={{0,1},{1,2},{2,3},{3,4},{4,5},{5,6},{6,7},{7,8},{8,9},{9,10},{10,1... | collective-permute-start | bytes 1572872 | tf_op jit(solution)/shard_map/while/body/eval_jaxpr/ppermute | solution.py:13
  273.9 10.8 %collective-permute-start = (f32[8,128,128]{2,1,0:T(8,128)S(1)}, f32[8,128,128]{2,1,0:T(8,128)S(1)}, u32[]{:S(2)}, u32[]{:S(2)}) collective-permute-start(f32[8,128,128]{2,1,0:T(8,128)S(1)} %get-tuple-element.265), channel_id=1, source_target_pairs={{0,1},{1,2},{2,3},{3,4},{4,5},{5,6},{6,7},{7,8},{8,9},{9,10},{10,1... | collective-permute-start | bytes 1572872 | tf_op jit(solution)/shard_map/while/body/eval_jaxpr/ppermute | solution.py:13
  293.5 10.8 %collective-permute-start = (f32[8,128,128]{2,1,0:T(8,128)S(1)}, f32[8,128,128]{2,1,0:T(8,128)S(1)}, u32[]{:S(2)}, u32[]{:S(2)}) collective-permute-start(f32[8,128,128]{2,1,0:T(8,128)S(1)} %get-tuple-element.265), channel_id=1, source_target_pairs={{0,1},{1,2},{2,3},{3,4},{4,5},{5,6},{6,7},{7,8},{8,9},{9,10},{10,1... | collective-permute-start | bytes 1572872 | tf_op jit(solution)/shard_map/while/body/eval_jaxpr/ppermute | solution.py:13
  313.2 10.8 %collective-permute-start = (f32[8,128,128]{2,1,0:T(8,128)S(1)}, f32[8,128,128]{2,1,0:T(8,128)S(1)}, u32[]{:S(2)}, u32[]{:S(2)}) collective-permute-start(f32[8,128,128]{2,1,0:T(8,128)S(1)} %get-tuple-element.265), channel_id=1, source_target_pairs={{0,1},{1,2},{2,3},{3,4},{4,5},{5,6},{6,7},{7,8},{8,9},{9,10},{10,1... | collective-permute-start | bytes 1572872 | tf_op jit(solution)/shard_map/while/body/eval_jaxpr/ppermute | solution.py:13
  332.8 10.8 %collective-permute-start = (f32[8,128,128]{2,1,0:T(8,128)S(1)}, f32[8,128,128]{2,1,0:T(8,128)S(1)}, u32[]{:S(2)}, u32[]{:S(2)}) collective-permute-start(f32[8,128,128]{2,1,0:T(8,128)S(1)} %get-tuple-element.265), channel_id=1, source_target_pairs={{0,1},{1,2},{2,3},{3,4},{4,5},{5,6},{6,7},{7,8},{8,9},{9,10},{10,1... | collective-permute-start | bytes 1572872 | tf_op jit(solution)/shard_map/while/body/eval_jaxpr/ppermute | solution.py:13
  352.5 10.8 %collective-permute-start = (f32[8,128,128]{2,1,0:T(8,128)S(1)}, f32[8,128,128]{2,1,0:T(8,128)S(1)}, u32[]{:S(2)}, u32[]{:S(2)}) collective-permute-start(f32[8,128,128]{2,1,0:T(8,128)S(1)} %get-tuple-element.265), channel_id=1, source_target_pairs={{0,1},{1,2},{2,3},{3,4},{4,5},{5,6},{6,7},{7,8},{8,9},{9,10},{10,1... | collective-permute-start | bytes 1572872 | tf_op jit(solution)/shard_map/while/body/eval_jaxpr/ppermute | solution.py:13
  372.1 10.8 %collective-permute-start = (f32[8,128,128]{2,1,0:T(8,128)S(1)}, f32[8,128,128]{2,1,0:T(8,128)S(1)}, u32[]{:S(2)}, u32[]{:S(2)}) collective-permute-start(f32[8,128,128]{2,1,0:T(8,128)S(1)} %get-tuple-element.265), channel_id=1, source_target_pairs={{0,1},{1,2},{2,3},{3,4},{4,5},{5,6},{6,7},{7,8},{8,9},{9,10},{10,1... | collective-permute-start | bytes 1572872 | tf_op jit(solution)/shard_map/while/body/eval_jaxpr/ppermute | solution.py:13
Sparse Core Ops, SparseCore 0:
  9.7 74.0 all-gather.1
where the time goes:
time: 402 us; the launch traced here: 401 us
  matrix products  237 us (59%)
  waiting for transfers between devices  122 us (30%)
  local copies, waits for them, and re-layouts  16 us (4%)
  between operations  13.5 us (3%)
  other arithmetic  9.96 us (2%)
    dot_general x16, matrix products, add_block(): jnp.einsum('gs,sij->gij', b_pick, b_all, precision=lax.Precision.HIGHEST,...  97 us
    dot_general x16, matrix products, add_block(): jnp.einsum('gij,gjk->gik', left_tiles, right_tiles, precision=lax.Precisi...  73.2 us
    all_gather x1, waiting for transfers between devices, body(): gathered_b = lax.all_gather(b_tiles, 'row', axis=0, tiled=True)  71.7 us
    ppermute x15, waiting for transfers between devices, shifted(): return lax.ppermute(value, axis, pairs)  50.3 us
    dot_general x16, matrix products, add_block(): jnp.einsum('mg,gik->mik', c_place, products, precision=lax.Precision.HIGH...  49.5 us
    dot_general x16, matrix products, add_block(): jnp.einsum('gs,sij->gij', a_pick, a_panel, precision=lax.Precision.HIGHES...  17.2 us
    dynamic_slice x16, local copies, waits for them, and re-layouts, visit(): lax.dynamic_index_in_dim(counts_all, panel_index, 0, keepdims=False)  10.2 us
    lt x16, other arithmetic, add_block(): is_live = jnp.arange(group_size, dtype=jnp.int32) < count_live  9.96 us
  transfers between devices with their start and end apart: 16, of which 16 were waited for; matrix products, arithmetic and copies ran while one was open for 28% of the time, Pallas kernels for 0%

commit v1 on v0

--- a/solution.py
+++ b/solution.py
@@ -66,7 +66,9 @@
     tile_width = a_tiles.shape[3]
     col_count = lax.axis_size("col")
     own_column = lax.axis_index("col")
-    gathered_b = lax.all_gather(b_tiles, "row", axis=0, tiled=True)
+    gathered_b = jnp.concatenate(
+        lax.all_to_all(jnp.stack([b_tiles] * lax.axis_size("row")), "row", 0, 0), axis=0
+    )
     b_all = gathered_b.reshape(-1, tile_width, tile_width)
     lists_all = pair_lists[0, 0]
     counts_all = stack_counts[0, 0]

time: 402 us -> 373 us (0.928)
  waiting for transfers between devices: 122 us -> 96.8 us
  between operations: 13.5 us -> 0.08 us
  starting transfers between devices: 1.12 us -> 9.28 us
    all_gather x1 -> x0, waiting for transfers between devices: 71.7 us -> none  [body(): gathered_b = lax.all_gather(b_tiles, 'row', axis=0, tiled=True)]
    all_to_all x0 -> x1, waiting for transfers between devices: none -> 46.6 us  [body(): lax.all_to_all(jnp.stack([b_tiles] * lax.axis_size('row')), 'row', 0, 0)]
    all_to_all x0 -> x1, starting transfers between devices: none -> 8.16 us  [body(): lax.all_to_all(jnp.stack([b_tiles] * lax.axis_size('row')), 'row', 0, 0)]
  transfers between devices with their start and end apart: 16 -> 16, of which waited for: 16 -> 16; matrix products, arithmetic and copies ran while one was open for 28% -> 30% of each run, Pallas kernels for 0% -> 0%
where the time goes in v1:
time: 373 us; the launch traced here: 372 us
  matrix products  237 us (64%)
  waiting for transfers between devices  96.8 us (26%)
  local copies, waits for them, and re-layouts  17.8 us (5%)
  other arithmetic  9.78 us (3%)
  starting transfers between devices  9.28 us (2%)
    dot_general x16, matrix products, add_block(): jnp.einsum('gs,sij->gij', b_pick, b_all, precision=lax.Precision.HIGHEST,...  97 us
    dot_general x16, matrix products, add_block(): jnp.einsum('gij,gjk->gik', left_tiles, right_tiles, precision=lax.Precisi...  73.2 us
    ppermute x15, waiting for transfers between devices, shifted(): return lax.ppermute(value, axis, pairs)  50.2 us
    dot_general x16, matrix products, add_block(): jnp.einsum('mg,gik->mik', c_place, products, precision=lax.Precision.HIGH...  49.5 us
    all_to_all x1, waiting for transfers between devices, body(): lax.all_to_all(jnp.stack([b_tiles] * lax.axis_size('row')), 'row', 0, 0)  46.6 us
    dot_general x16, matrix products, add_block(): jnp.einsum('gs,sij->gij', a_pick, a_panel, precision=lax.Precision.HIGHES...  17.2 us
    dynamic_slice x16, local copies, waits for them, and re-layouts, visit(): lax.dynamic_index_in_dim(counts_all, panel_index, 0, keepdims=False)  9.92 us
    lt x16, other arithmetic, add_block(): is_live = jnp.arange(group_size, dtype=jnp.int32) < count_live  9.78 us
  transfers between devices with their start and end apart: 16, of which 16 were waited for; matrix products, arithmetic and copies ran while one was open for 30% of the time, Pallas kernels for 0%

profile of v1, /device:TPU:0, one launch (start us, length us, event | category | flops | bytes accessed | tf_op | source)
XLA Modules:
  0.0 372.2 jit_solution(4315702813916285630)
XLA Ops:
  4.6 8.2 %all-to-all-start = ((f32[8,1,1,8,128,128]{5,4,3,2,1,0:T(8,128)}), f32[8,1,1,8,128,128]{5,4,3,2,1,0:T(8,128)}, u32[]{:S(2)}, u32[]{:S(2)}) async-start(f32[8,1,1,8,128,128]{5,4,3,2,1,0:T(8,128)} %stack.2), calls=%async_computation | async-start | bytes 8388608 | tf_op jit(solution)/shard_map/all_to_all | solution.py:70
  15.2 46.6 %all-to-all-done = f32[8,1,1,8,128,128]{5,4,3,2,1,0:T(8,128)} async-done(((f32[8,1,1,8,128,128]{5,4,3,2,1,0:T(8,128)}), f32[8,1,1,8,128,128]{5,4,3,2,1,0:T(8,128)}, u32[]{:S(2)}, u32[]{:S(2)}) %all-to-all-start) | async-done | bytes 4194336 | tf_op jit(solution)/shard_map/all_to_all | solution.py:70
  61.8 6.1 %fusion.23 = f32[32,128,128]{2,0,1:T(8,128)S(1)} fusion(f32[64,128,128]{2,1,0:T(8,128)} %bitcast.16, s32[32]{0:T(128)S(1)} %get-tuple-element.202), kind=kOutput, calls=%fused_computation.26 | convolution fusion | flops 402655232 | bytes 6291584 | tf_op jit(solution)/shard_map/gs,sij->gij/dot_general | solution.py:35
  74.8 294.9 %while.17 = (s32[]{:T(128)}, f32[32,128,128]{2,0,1:T(8,128)S(1)}, f32[8,128,128]{2,1,0:T(8,128)S(1)}, s32[]{:T(128)}, s32[16,3,32]{2,1,0:T(4,128)S(1)}, /*index=...) while((s32[]{:T(128)}, f32[32,128,128]{2,0,1:T(8,128)S(1)}, ...), condition=%wide.region_1.2_spmd, body=%wide.region_0.1_spmd.sunk | while | flops 1460146432 | bytes 24643844 | solution.py:93
  76.4 6.1 %fusion.66 = f32[32,128,128]{2,0,1:T(8,128)S(1)} fusion(f32[64,128,128]{2,1,0:T(8,128)} %get-tuple-element.280, s32[32]{0:T(128)S(1)} %get-tuple-element.249), kind=kOutput, calls=%fused_computation.clone.1 | convolution fusion | flops 402655232 | bytes 6291584 | tf_op jit(solution)/shard_map/while/body/eval_jaxpr/gs,sij->gij/dot_general | solution.py:35
  86.9 4.6 %fusion.68 = f32[32,128,128]{2,1,0:T(8,128)S(1)} fusion(f32[32,128,128]{2,0,1:T(8,128)S(1)} %fusion.66, f32[32,128,128]{2,0,1:T(8,128)S(1)} %fusion.67), kind=kOutput, calls=%fused_computation.4.clone.1 | convolution fusion | flops 805306368 | bytes 6291456 | tf_op jit(solution)/shard_map/while/body/eval_jaxpr/gij,gjk->gik/dot_general | solution.py:42
  96.0 6.1 %fusion.66 = f32[32,128,128]{2,0,1:T(8,128)S(1)} fusion(f32[64,128,128]{2,1,0:T(8,128)} %get-tuple-element.280, s32[32]{0:T(128)S(1)} %get-tuple-element.249), kind=kOutput, calls=%fused_computation.clone.1 | convolution fusion | flops 402655232 | bytes 6291584 | tf_op jit(solution)/shard_map/while/body/eval_jaxpr/gs,sij->gij/dot_general | solution.py:35
  106.5 4.6 %fusion.68 = f32[32,128,128]{2,1,0:T(8,128)S(1)} fusion(f32[32,128,128]{2,0,1:T(8,128)S(1)} %fusion.66, f32[32,128,128]{2,0,1:T(8,128)S(1)} %fusion.67), kind=kOutput, calls=%fused_computation.4.clone.1 | convolution fusion | flops 805306368 | bytes 6291456 | tf_op jit(solution)/shard_map/while/body/eval_jaxpr/gij,gjk->gik/dot_general | solution.py:42
  115.7 6.1 %fusion.66 = f32[32,128,128]{2,0,1:T(8,128)S(1)} fusion(f32[64,128,128]{2,1,0:T(8,128)} %get-tuple-element.280, s32[32]{0:T(128)S(1)} %get-tuple-element.249), kind=kOutput, calls=%fused_computation.clone.1 | convolution fusion | flops 402655232 | bytes 6291584 | tf_op jit(solution)/shard_map/while/body/eval_jaxpr/gs,sij->gij/dot_general | solution.py:35
  126.2 4.6 %fusion.68 = f32[32,128,128]{2,1,0:T(8,128)S(1)} fusion(f32[32,128,128]{2,0,1:T(8,128)S(1)} %fusion.66, f32[32,128,128]{2,0,1:T(8,128)S(1)} %fusion.67), kind=kOutput, calls=%fused_computation.4.clone.1 | convolution fusion | flops 805306368 | bytes 6291456 | tf_op jit(solution)/shard_map/while/body/eval_jaxpr/gij,gjk->gik/dot_general | solution.py:42
  135.3 6.1 %fusion.66 = f32[32,128,128]{2,0,1:T(8,128)S(1)} fusion(f32[64,128,128]{2,1,0:T(8,128)} %get-tuple-element.280, s32[32]{0:T(128)S(1)} %get-tuple-element.249), kind=kOutput, calls=%fused_computation.clone.1 | convolution fusion | flops 402655232 | bytes 6291584 | tf_op jit(solution)/shard_map/while/body/eval_jaxpr/gs,sij->gij/dot_general | solution.py:35
  145.8 4.6 %fusion.68 = f32[32,128,128]{2,1,0:T(8,128)S(1)} fusion(f32[32,128,128]{2,0,1:T(8,128)S(1)} %fusion.66, f32[32,128,128]{2,0,1:T(8,128)S(1)} %fusion.67), kind=kOutput, calls=%fused_computation.4.clone.1 | convolution fusion | flops 805306368 | bytes 6291456 | tf_op jit(solution)/shard_map/while/body/eval_jaxpr/gij,gjk->gik/dot_general | solution.py:42
  155.0 6.1 %fusion.66 = f32[32,128,128]{2,0,1:T(8,128)S(1)} fusion(f32[64,128,128]{2,1,0:T(8,128)} %get-tuple-element.280, s32[32]{0:T(128)S(1)} %get-tuple-element.249), kind=kOutput, calls=%fused_computation.clone.1 | convolution fusion | flops 402655232 | bytes 6291584 | tf_op jit(solution)/shard_map/while/body/eval_jaxpr/gs,sij->gij/dot_general | solution.py:35
  165.5 4.6 %fusion.68 = f32[32,128,128]{2,1,0:T(8,128)S(1)} fusion(f32[32,128,128]{2,0,1:T(8,128)S(1)} %fusion.66, f32[32,128,128]{2,0,1:T(8,128)S(1)} %fusion.67), kind=kOutput, calls=%fused_computation.4.clone.1 | convolution fusion | flops 805306368 | bytes 6291456 | tf_op jit(solution)/shard_map/while/body/eval_jaxpr/gij,gjk->gik/dot_general | solution.py:42
  174.6 6.1 %fusion.66 = f32[32,128,128]{2,0,1:T(8,128)S(1)} fusion(f32[64,128,128]{2,1,0:T(8,128)} %get-tuple-element.280, s32[32]{0:T(128)S(1)} %get-tuple-element.249), kind=kOutput, calls=%fused_computation.clone.1 | convolution fusion | flops 402655232 | bytes 6291584 | tf_op jit(solution)/shard_map/while/body/eval_jaxpr/gs,sij->gij/dot_general | solution.py:35
  185.1 4.6 %fusion.68 = f32[32,128,128]{2,1,0:T(8,128)S(1)} fusion(f32[32,128,128]{2,0,1:T(8,128)S(1)} %fusion.66, f32[32,128,128]{2,0,1:T(8,128)S(1)} %fusion.67), kind=kOutput, calls=%fused_computation.4.clone.1 | convolution fusion | flops 805306368 | bytes 6291456 | tf_op jit(solution)/shard_map/while/body/eval_jaxpr/gij,gjk->gik/dot_general | solution.py:42
  194.3 6.1 %fusion.66 = f32[32,128,128]{2,0,1:T(8,128)S(1)} fusion(f32[64,128,128]{2,1,0:T(8,128)} %get-tuple-element.280, s32[32]{0:T(128)S(1)} %get-tuple-element.249), kind=kOutput, calls=%fused_computation.clone.1 | convolution fusion | flops 402655232 | bytes 6291584 | tf_op jit(solution)/shard_map/while/body/eval_jaxpr/gs,sij->gij/dot_general | solution.py:35
  204.8 4.6 %fusion.68 = f32[32,128,128]{2,1,0:T(8,128)S(1)} fusion(f32[32,128,128]{2,0,1:T(8,128)S(1)} %fusion.66, f32[32,128,128]{2,0,1:T(8,128)S(1)} %fusion.67), kind=kOutput, calls=%fused_computation.4.clone.1 | convolution fusion | flops 805306368 | bytes 6291456 | tf_op jit(solution)/shard_map/while/body/eval_jaxpr/gij,gjk->gik/dot_general | solution.py:42
  213.9 6.1 %fusion.66 = f32[32,128,128]{2,0,1:T(8,128)S(1)} fusion(f32[64,128,128]{2,1,0:T(8,128)} %get-tuple-element.280, s32[32]{0:T(128)S(1)} %get-tuple-element.249), kind=kOutput, calls=%fused_computation.clone.1 | convolution fusion | flops 402655232 | bytes 6291584 | tf_op jit(solution)/shard_map/while/body/eval_jaxpr/gs,sij->gij/dot_general | solution.py:35
  224.4 4.6 %fusion.68 = f32[32,128,128]{2,1,0:T(8,128)S(1)} fusion(f32[32,128,128]{2,0,1:T(8,128)S(1)} %fusion.66, f32[32,128,128]{2,0,1:T(8,128)S(1)} %fusion.67), kind=kOutput, calls=%fused_computation.4.clone.1 | convolution fusion | flops 805306368 | bytes 6291456 | tf_op jit(solution)/shard_map/while/body/eval_jaxpr/gij,gjk->gik/dot_general | solution.py:42
  233.6 6.1 %fusion.66 = f32[32,128,128]{2,0,1:T(8,128)S(1)} fusion(f32[64,128,128]{2,1,0:T(8,128)} %get-tuple-element.280, s32[32]{0:T(128)S(1)} %get-tuple-element.249), kind=kOutput, calls=%fused_computation.clone.1 | convolution fusion | flops 402655232 | bytes 6291584 | tf_op jit(solution)/shard_map/while/body/eval_jaxpr/gs,sij->gij/dot_general | solution.py:35
  244.0 4.6 %fusion.68 = f32[32,128,128]{2,1,0:T(8,128)S(1)} fusion(f32[32,128,128]{2,0,1:T(8,128)S(1)} %fusion.66, f32[32,128,128]{2,0,1:T(8,128)S(1)} %fusion.67), kind=kOutput, calls=%fused_computation.4.clone.1 | convolution fusion | flops 805306368 | bytes 6291456 | tf_op jit(solution)/shard_map/while/body/eval_jaxpr/gij,gjk->gik/dot_general | solution.py:42
  253.2 6.1 %fusion.66 = f32[32,128,128]{2,0,1:T(8,128)S(1)} fusion(f32[64,128,128]{2,1,0:T(8,128)} %get-tuple-element.280, s32[32]{0:T(128)S(1)} %get-tuple-element.249), kind=kOutput, calls=%fused_computation.clone.1 | convolution fusion | flops 402655232 | bytes 6291584 | tf_op jit(solution)/shard_map/while/body/eval_jaxpr/gs,sij->gij/dot_general | solution.py:35
  263.7 4.6 %fusion.68 = f32[32,128,128]{2,1,0:T(8,128)S(1)} fusion(f32[32,128,128]{2,0,1:T(8,128)S(1)} %fusion.66, f32[32,128,128]{2,0,1:T(8,128)S(1)} %fusion.67), kind=kOutput, calls=%fused_computation.4.clone.1 | convolution fusion | flops 805306368 | bytes 6291456 | tf_op jit(solution)/shard_map/while/body/eval_jaxpr/gij,gjk->gik/dot_general | solution.py:42
  272.8 6.1 %fusion.66 = f32[32,128,128]{2,0,1:T(8,128)S(1)} fusion(f32[64,128,128]{2,1,0:T(8,128)} %get-tuple-element.280, s32[32]{0:T(128)S(1)} %get-tuple-element.249), kind=kOutput, calls=%fused_computation.clone.1 | convolution fusion | flops 402655232 | bytes 6291584 | tf_op jit(solution)/shard_map/while/body/eval_jaxpr/gs,sij->gij/dot_general | solution.py:35
  283.3 4.6 %fusion.68 = f32[32,128,128]{2,1,0:T(8,128)S(1)} fusion(f32[32,128,128]{2,0,1:T(8,128)S(1)} %fusion.66, f32[32,128,128]{2,0,1:T(8,128)S(1)} %fusion.67), kind=kOutput, calls=%fused_computation.4.clone.1 | convolution fusion | flops 805306368 | bytes 6291456 | tf_op jit(solution)/shard_map/while/body/eval_jaxpr/gij,gjk->gik/dot_general | solution.py:42
  292.5 6.1 %fusion.66 = f32[32,128,128]{2,0,1:T(8,128)S(1)} fusion(f32[64,128,128]{2,1,0:T(8,128)} %get-tuple-element.280, s32[32]{0:T(128)S(1)} %get-tuple-element.249), kind=kOutput, calls=%fused_computation.clone.1 | convolution fusion | flops 402655232 | bytes 6291584 | tf_op jit(solution)/shard_map/while/body/eval_jaxpr/gs,sij->gij/dot_general | solution.py:35
  312.1 6.1 %fusion.66 = f32[32,128,128]{2,0,1:T(8,128)S(1)} fusion(f32[64,128,128]{2,1,0:T(8,128)} %get-tuple-element.280, s32[32]{0:T(128)S(1)} %get-tuple-element.249), kind=kOutput, calls=%fused_computation.clone.1 | convolution fusion | flops 402655232 | bytes 6291584 | tf_op jit(solution)/shard_map/while/body/eval_jaxpr/gs,sij->gij/dot_general | solution.py:35
  331.8 6.1 %fusion.66 = f32[32,128,128]{2,0,1:T(8,128)S(1)} fusion(f32[64,128,128]{2,1,0:T(8,128)} %get-tuple-element.280, s32[32]{0:T(128)S(1)} %get-tuple-element.249), kind=kOutput, calls=%fused_computation.clone.1 | convolution fusion | flops 402655232 | bytes 6291584 | tf_op jit(solution)/shard_map/while/body/eval_jaxpr/gs,sij->gij/dot_general | solution.py:35
  342.3 4.6 %fusion.68 = f32[32,128,128]{2,1,0:T(8,128)S(1)} fusion(f32[32,128,128]{2,0,1:T(8,128)S(1)} %fusion.66, f32[32,128,128]{2,0,1:T(8,128)S(1)} %fusion.67), kind=kOutput, calls=%fused_computation.4.clone.1 | convolution fusion | flops 805306368 | bytes 6291456 | tf_op jit(solution)/shard_map/while/body/eval_jaxpr/gij,gjk->gik/dot_general | solution.py:42
  351.4 6.1 %fusion.66 = f32[32,128,128]{2,0,1:T(8,128)S(1)} fusion(f32[64,128,128]{2,1,0:T(8,128)} %get-tuple-element.280, s32[32]{0:T(128)S(1)} %get-tuple-element.249), kind=kOutput, calls=%fused_computation.clone.1 | convolution fusion | flops 402655232 | bytes 6291584 | tf_op jit(solution)/shard_map/while/body/eval_jaxpr/gs,sij->gij/dot_general | solution.py:35
  361.9 4.6 %fusion.68 = f32[32,128,128]{2,1,0:T(8,128)S(1)} fusion(f32[32,128,128]{2,0,1:T(8,128)S(1)} %fusion.66, f32[32,128,128]{2,0,1:T(8,128)S(1)} %fusion.67), kind=kOutput, calls=%fused_computation.4.clone.1 | convolution fusion | flops 805306368 | bytes 6291456 | tf_op jit(solution)/shard_map/while/body/eval_jaxpr/gij,gjk->gik/dot_general | solution.py:42
  (151 shorter events, 159.3 us)
Async XLA Ops:
  4.6 8.2 %copy-start = (s32[1,1,16,3,32]{4,2,3,1,0:T(8,128)S(1)}, s32[1,1,16,3,32]{4,2,3,1,0:T(8,128)}, u32[]{:S(2)}) copy-start(s32[1,1,16,3,32]{4,2,3,1,0:T(8,128)} %param.8) | copy-start | bytes 18436
  4.6 8.2 %copy-start.1 = (s32[1,1,16]{2,1,0:T(1,128)S(1)}, s32[1,1,16]{2,1,0:T(1,128)}, u32[]{:S(2)}) copy-start(s32[1,1,16]{2,1,0:T(1,128)} %param.9) | copy-start | bytes 196
  4.6 57.1 %all-to-all-start = ((f32[8,1,1,8,128,128]{5,4,3,2,1,0:T(8,128)}), f32[8,1,1,8,128,128]{5,4,3,2,1,0:T(8,128)}, u32[]{:S(2)}, u32[]{:S(2)}) async-start(f32[8,1,1,8,128,128]{5,4,3,2,1,0:T(8,128)} %stack.2), calls=%async_computation | async-start | bytes 8388608 | tf_op jit(solution)/shard_map/all_to_all | solution.py:70
  75.0 10.8 %collective-permute-start = (f32[8,128,128]{2,1,0:T(8,128)S(1)}, f32[8,128,128]{2,1,0:T(8,128)S(1)}, u32[]{:S(2)}, u32[]{:S(2)}) collective-permute-start(f32[8,128,128]{2,1,0:T(8,128)S(1)} %get-tuple-element.265), channel_id=1, source_target_pairs={{0,1},{1,2},{2,3},{3,4},{4,5},{5,6},{6,7},{7,8},{8,9},{9,10},{10,1... | collective-permute-start | bytes 1572872 | tf_op jit(solution)/shard_map/while/body/eval_jaxpr/ppermute | solution.py:13
  94.7 10.8 %collective-permute-start = (f32[8,128,128]{2,1,0:T(8,128)S(1)}, f32[8,128,128]{2,1,0:T(8,128)S(1)}, u32[]{:S(2)}, u32[]{:S(2)}) collective-permute-start(f32[8,128,128]{2,1,0:T(8,128)S(1)} %get-tuple-element.265), channel_id=1, source_target_pairs={{0,1},{1,2},{2,3},{3,4},{4,5},{5,6},{6,7},{7,8},{8,9},{9,10},{10,1... | collective-permute-start | bytes 1572872 | tf_op jit(solution)/shard_map/while/body/eval_jaxpr/ppermute | solution.py:13
  114.3 10.8 %collective-permute-start = (f32[8,128,128]{2,1,0:T(8,128)S(1)}, f32[8,128,128]{2,1,0:T(8,128)S(1)}, u32[]{:S(2)}, u32[]{:S(2)}) collective-permute-start(f32[8,128,128]{2,1,0:T(8,128)S(1)} %get-tuple-element.265), channel_id=1, source_target_pairs={{0,1},{1,2},{2,3},{3,4},{4,5},{5,6},{6,7},{7,8},{8,9},{9,10},{10,1... | collective-permute-start | bytes 1572872 | tf_op jit(solution)/shard_map/while/body/eval_jaxpr/ppermute | solution.py:13
  134.0 10.8 %collective-permute-start = (f32[8,128,128]{2,1,0:T(8,128)S(1)}, f32[8,128,128]{2,1,0:T(8,128)S(1)}, u32[]{:S(2)}, u32[]{:S(2)}) collective-permute-start(f32[8,128,128]{2,1,0:T(8,128)S(1)} %get-tuple-element.265), channel_id=1, source_target_pairs={{0,1},{1,2},{2,3},{3,4},{4,5},{5,6},{6,7},{7,8},{8,9},{9,10},{10,1... | collective-permute-start | bytes 1572872 | tf_op jit(solution)/shard_map/while/body/eval_jaxpr/ppermute | solution.py:13
  153.6 10.8 %collective-permute-start = (f32[8,128,128]{2,1,0:T(8,128)S(1)}, f32[8,128,128]{2,1,0:T(8,128)S(1)}, u32[]{:S(2)}, u32[]{:S(2)}) collective-permute-start(f32[8,128,128]{2,1,0:T(8,128)S(1)} %get-tuple-element.265), channel_id=1, source_target_pairs={{0,1},{1,2},{2,3},{3,4},{4,5},{5,6},{6,7},{7,8},{8,9},{9,10},{10,1... | collective-permute-start | bytes 1572872 | tf_op jit(solution)/shard_map/while/body/eval_jaxpr/ppermute | solution.py:13
  173.2 10.8 %collective-permute-start = (f32[8,128,128]{2,1,0:T(8,128)S(1)}, f32[8,128,128]{2,1,0:T(8,128)S(1)}, u32[]{:S(2)}, u32[]{:S(2)}) collective-permute-start(f32[8,128,128]{2,1,0:T(8,128)S(1)} %get-tuple-element.265), channel_id=1, source_target_pairs={{0,1},{1,2},{2,3},{3,4},{4,5},{5,6},{6,7},{7,8},{8,9},{9,10},{10,1... | collective-permute-start | bytes 1572872 | tf_op jit(solution)/shard_map/while/body/eval_jaxpr/ppermute | solution.py:13
  192.9 10.8 %collective-permute-start = (f32[8,128,128]{2,1,0:T(8,128)S(1)}, f32[8,128,128]{2,1,0:T(8,128)S(1)}, u32[]{:S(2)}, u32[]{:S(2)}) collective-permute-start(f32[8,128,128]{2,1,0:T(8,128)S(1)} %get-tuple-element.265), channel_id=1, source_target_pairs={{0,1},{1,2},{2,3},{3,4},{4,5},{5,6},{6,7},{7,8},{8,9},{9,10},{10,1... | collective-permute-start | bytes 1572872 | tf_op jit(solution)/shard_map/while/body/eval_jaxpr/ppermute | solution.py:13
  212.5 10.8 %collective-permute-start = (f32[8,128,128]{2,1,0:T(8,128)S(1)}, f32[8,128,128]{2,1,0:T(8,128)S(1)}, u32[]{:S(2)}, u32[]{:S(2)}) collective-permute-start(f32[8,128,128]{2,1,0:T(8,128)S(1)} %get-tuple-element.265), channel_id=1, source_target_pairs={{0,1},{1,2},{2,3},{3,4},{4,5},{5,6},{6,7},{7,8},{8,9},{9,10},{10,1... | collective-permute-start | bytes 1572872 | tf_op jit(solution)/shard_map/while/body/eval_jaxpr/ppermute | solution.py:13
  232.2 10.8 %collective-permute-start = (f32[8,128,128]{2,1,0:T(8,128)S(1)}, f32[8,128,128]{2,1,0:T(8,128)S(1)}, u32[]{:S(2)}, u32[]{:S(2)}) collective-permute-start(f32[8,128,128]{2,1,0:T(8,128)S(1)} %get-tuple-element.265), channel_id=1, source_target_pairs={{0,1},{1,2},{2,3},{3,4},{4,5},{5,6},{6,7},{7,8},{8,9},{9,10},{10,1... | collective-permute-start | bytes 1572872 | tf_op jit(solution)/shard_map/while/body/eval_jaxpr/ppermute | solution.py:13
  251.8 10.8 %collective-permute-start = (f32[8,128,128]{2,1,0:T(8,128)S(1)}, f32[8,128,128]{2,1,0:T(8,128)S(1)}, u32[]{:S(2)}, u32[]{:S(2)}) collective-permute-start(f32[8,128,128]{2,1,0:T(8,128)S(1)} %get-tuple-element.265), channel_id=1, source_target_pairs={{0,1},{1,2},{2,3},{3,4},{4,5},{5,6},{6,7},{7,8},{8,9},{9,10},{10,1... | collective-permute-start | bytes 1572872 | tf_op jit(solution)/shard_map/while/body/eval_jaxpr/ppermute | solution.py:13
  271.5 10.8 %collective-permute-start = (f32[8,128,128]{2,1,0:T(8,128)S(1)}, f32[8,128,128]{2,1,0:T(8,128)S(1)}, u32[]{:S(2)}, u32[]{:S(2)}) collective-permute-start(f32[8,128,128]{2,1,0:T(8,128)S(1)} %get-tuple-element.265), channel_id=1, source_target_pairs={{0,1},{1,2},{2,3},{3,4},{4,5},{5,6},{6,7},{7,8},{8,9},{9,10},{10,1... | collective-permute-start | bytes 1572872 | tf_op jit(solution)/shard_map/while/body/eval_jaxpr/ppermute | solution.py:13
  291.1 10.8 %collective-permute-start = (f32[8,128,128]{2,1,0:T(8,128)S(1)}, f32[8,128,128]{2,1,0:T(8,128)S(1)}, u32[]{:S(2)}, u32[]{:S(2)}) collective-permute-start(f32[8,128,128]{2,1,0:T(8,128)S(1)} %get-tuple-element.265), channel_id=1, source_target_pairs={{0,1},{1,2},{2,3},{3,4},{4,5},{5,6},{6,7},{7,8},{8,9},{9,10},{10,1... | collective-permute-start | bytes 1572872 | tf_op jit(solution)/shard_map/while/body/eval_jaxpr/ppermute | solution.py:13
  310.8 10.8 %collective-permute-start = (f32[8,128,128]{2,1,0:T(8,128)S(1)}, f32[8,128,128]{2,1,0:T(8,128)S(1)}, u32[]{:S(2)}, u32[]{:S(2)}) collective-permute-start(f32[8,128,128]{2,1,0:T(8,128)S(1)} %get-tuple-element.265), channel_id=1, source_target_pairs={{0,1},{1,2},{2,3},{3,4},{4,5},{5,6},{6,7},{7,8},{8,9},{9,10},{10,1... | collective-permute-start | bytes 1572872 | tf_op jit(solution)/shard_map/while/body/eval_jaxpr/ppermute | solution.py:13
  330.4 10.8 %collective-permute-start = (f32[8,128,128]{2,1,0:T(8,128)S(1)}, f32[8,128,128]{2,1,0:T(8,128)S(1)}, u32[]{:S(2)}, u32[]{:S(2)}) collective-permute-start(f32[8,128,128]{2,1,0:T(8,128)S(1)} %get-tuple-element.265), channel_id=1, source_target_pairs={{0,1},{1,2},{2,3},{3,4},{4,5},{5,6},{6,7},{7,8},{8,9},{9,10},{10,1... | collective-permute-start | bytes 1572872 | tf_op jit(solution)/shard_map/while/body/eval_jaxpr/ppermute | solution.py:13
  350.1 10.8 %collective-permute-start = (f32[8,128,128]{2,1,0:T(8,128)S(1)}, f32[8,128,128]{2,1,0:T(8,128)S(1)}, u32[]{:S(2)}, u32[]{:S(2)}) collective-permute-start(f32[8,128,128]{2,1,0:T(8,128)S(1)} %get-tuple-element.265), channel_id=1, source_target_pairs={{0,1},{1,2},{2,3},{3,4},{4,5},{5,6},{6,7},{7,8},{8,9},{9,10},{10,1... | collective-permute-start | bytes 1572872 | tf_op jit(solution)/shard_map/while/body/eval_jaxpr/ppermute | solution.py:13
